TPU v7x, 128 devices: a whole 4x4x4 slice. The times are simulated.
128 devices in a mesh: blk: 4 (over z), own: 32 (over y, x, core).
Axes of the slice: x: 4, y: 4, z: 4, core: 2. Of those that a mesh axis runs over, the one named last changes fastest.
Arguments:
- blocks: bfloat16 [512, 128, 16384], P(('blk', 'own')), may hold values from -6 to 6
- user_block: int32 [512], P(('blk', 'own')), may hold values from 0 to 63, as said below
- item_block: int32 [512], P(('blk', 'own')), may hold values from 0 to 15, as said below
- word_block: int32 [512], P(('blk', 'own')), may hold values from 0 to 31, as said below
- item_factor: bfloat16 [2048, 256], P('blk')
- word_factor: bfloat16 [4096, 256], replicated
Outputs:
- user_factor: float32 [128, 64, 256], P('own', 'blk')
Inputs may be any that keep to these rules, and one draw needn't show every extreme that they name: `user_block`: every user block appears exactly 8 times in the list. `item_block`: every item block appears in the list. `word_block`: every word block appears in the list.
All inputs are finite; a program needn't handle non-finite values.
Results may differ from a plain program's by a relative error of at most 0.0036.
Values may be sent and summed in bfloat16 or wider, within the bound.
A program may use at most 128 MiB of HBM per device.

v0:
```python
import jax
import jax.numpy as jnp
from jax import lax
from jax.sharding import PartitionSpec as P

BLOCKS_PER_USER = 8


def block_term(item_rows, word_rows, block):
    count = item_rows.shape[0]
    khatri = item_rows.astype(jnp.float32)[:, None, :] * word_rows.astype(jnp.float32)[None, :, :]
    khatri = khatri.astype(jnp.bfloat16).reshape(count * word_rows.shape[0], item_rows.shape[1])
    return jnp.dot(block, khatri, preferred_element_type=jnp.float32)


def factorize(matrix):
    order = matrix.shape[0]
    places = jnp.arange(order, dtype=jnp.int32)

    def column_step(index, lower):
        row_now = lax.dynamic_slice_in_dim(lower, index, 1, 0)[0]
        target = lax.dynamic_slice_in_dim(matrix, index, 1, 1)[:, 0]
        diag_value = jnp.sqrt(
            jnp.sum(jnp.where(places == index, target, 0.0)) - jnp.sum(row_now * row_now)
        )
        column = (target - jnp.dot(lower, row_now, precision=lax.Precision.HIGHEST)) / diag_value
        column = jnp.where(places > index, column, jnp.where(places == index, diag_value, 0.0))
        return lax.dynamic_update_slice_in_dim(lower, column[:, None], index, 1)

    return lax.fori_loop(0, order, column_step, jnp.zeros((order, order), jnp.float32))


def solve_rows(lower, values):
    order = lower.shape[0]
    places = jnp.arange(order, dtype=jnp.int32)

    def forward_step(index, solved):
        row_now = lax.dynamic_slice_in_dim(lower, index, 1, 0)[0]
        pivot = jnp.sum(jnp.where(places == index, row_now, 0.0))
        given = lax.dynamic_slice_in_dim(values, index, 1, 1)[:, 0]
        fresh = (given - jnp.dot(solved, row_now, precision=lax.Precision.HIGHEST)) / pivot
        return lax.dynamic_update_slice_in_dim(solved, fresh[:, None], index, 1)

    middle = lax.fori_loop(0, order, forward_step, jnp.zeros_like(values))

    def backward_step(count, solved):
        index = order - 1 - count
        column = lax.dynamic_slice_in_dim(lower, index, 1, 1)[:, 0]
        pivot = jnp.sum(jnp.where(places == index, column, 0.0))
        below = jnp.where(places > index, column, 0.0)
        given = lax.dynamic_slice_in_dim(middle, index, 1, 1)[:, 0]
        fresh = (given - jnp.dot(solved, below, precision=lax.Precision.HIGHEST)) / pivot
        return lax.dynamic_update_slice_in_dim(solved, fresh[:, None], index, 1)

    return lax.fori_loop(0, order, backward_step, jnp.zeros_like(values))


def on_device(blocks, user_block, item_block, word_block, item_factor, word_factor):
    nblocks = blocks.shape[0]
    side = blocks.shape[1]
    rank = item_factor.shape[1]
    owners = lax.axis_size("own")
    groups = lax.axis_size("blk")
    ublocks = nblocks * groups * owners // BLOCKS_PER_USER
    row_share = side // owners
    word_rows = [
        lax.dynamic_slice_in_dim(word_factor, word_block[n] * side, side, 0) for n in range(nblocks)
    ]

    def skipped(item_rows, words, block):
        return jnp.zeros((side, rank), jnp.float32)

    start_rows = jnp.zeros((nblocks, side, rank), jnp.float32)
    start_gram = jnp.zeros((rank, rank), jnp.float32)
    piece = lax.all_gather(item_factor, "blk", axis=0, tiled=True)
    accumulate_partial_rows = start_rows
    gram_items = start_gram
    length = piece.shape[0]
    padded = jnp.pad(piece, ((side, side), (0, 0)))
    for n in range(nblocks):
        offset = item_block[n] * side
        present = jnp.logical_and(offset < length, offset + side > 0)
        first = jnp.clip(offset + side, 0, length + side)
        item_rows = lax.dynamic_slice_in_dim(padded, first, side, 0)
        added = lax.cond(present, block_term, skipped, item_rows, word_rows[n], blocks[n])
        accumulate_partial_rows = accumulate_partial_rows.at[n].add(added)
    partial_rows, gram_items = (accumulate_partial_rows, gram_items)
    gram_items = lax.psum(
        jnp.dot(item_factor.T, item_factor, preferred_element_type=jnp.float32), "blk"
    )
    gram_words = jnp.dot(word_factor.T, word_factor, preferred_element_type=jnp.float32)
    gram = gram_items * gram_words
    selector = (jnp.arange(ublocks, dtype=jnp.int32)[:, None] == user_block[None, :]).astype(
        jnp.float32
    )
    owned = lax.psum_scatter(
        jnp.einsum("un,nqr->qur", selector, partial_rows, precision=lax.Precision.HIGHEST),
        "own",
        scatter_dimension=0,
        tiled=True,
    )
    mttkrp = lax.psum_scatter(owned, "blk", scatter_dimension=1, tiled=True)
    local_count = mttkrp.shape[1]
    lower = factorize(gram)
    stacked = mttkrp.reshape(row_share * local_count, rank)
    solved = solve_rows(lower, stacked)
    return solved.reshape(row_share, local_count, rank)


def solution(mesh):
    return jax.shard_map(
        on_device,
        mesh=mesh,
        in_specs=(
            P(("blk", "own"), None, None),
            P(("blk", "own")),
            P(("blk", "own")),
            P(("blk", "own")),
            P("blk", None),
            P(),
        ),
        out_specs=P("own", "blk", None),
        check_vma=False,
    )
```

profile of v0, /device:TPU:1, one launch (start us, length us, event | category | flops | bytes accessed | tf_op | source)
XLA Modules:
  0.0 1767.6 jit_solution(16234740604607590884)
XLA Ops:
  7.3 2.0 fusion.50
  9.4 1.5 fusion.49
  13.4 22.2 %all-gather.2.cloned.1.call-done = bf16[2048,256]{1,0:T(8,128)(2,1)} async-done(((bf16[512,256]{1,0:T(8,128)(2,1)}), bf16[2048,256]{1,0:T(8,128)(2,1)}) %all-gather.2.cloned.1.call-update) | async-done | bytes 1048592 | tf_op jit(solution)/shard_map/all_gather | solution.py:75
  35.6 1.3 pad.16
  36.9 9.8 conditional.4
  37.5 0.9 dynamic-slice_convert_fusion
  38.4 3.5 multiply_convert_fusion
  41.9 4.6 fusion.9
  46.6 11.0 conditional.5
  46.7 1.2 slice.127
  48.6 0.9 dynamic-slice_convert_fusion.2
  49.4 3.5 multiply_convert_fusion.1
  53.0 4.7 fusion.15
  57.7 11.2 conditional.6
  57.9 1.2 slice.129
  59.8 0.9 dynamic-slice_convert_fusion.4
  60.6 3.5 multiply_convert_fusion.2
  64.2 4.6 fusion.21
  68.9 11.0 conditional.7
  68.9 1.2 slice.131
  70.8 0.9 dynamic-slice_convert_fusion.6
  71.7 3.5 multiply_convert_fusion.3
  75.2 4.7 fusion.27
  80.2 5.9 convolution_bitcast_fusion.2
  86.2 1.7 convolution_multiply_fusion
  88.0 90.4 %reduce-scatter.3.cloned.1.call-done = f32[4,64,256]{2,1,0:T(8,128)} async-done(((f32[128,64,256]{2,1,0:T(8,128)}), f32[4,64,256]{2,1,0:T(8,128)}) %reduce-scatter.3.cloned.1.call-update) | async-done | bytes 262160 | tf_op jit(solution)/shard_map/reduce_scatter | solution.py:96
  178.5 798.1 %while.51 = (s32[]{:T(128)}, f32[256,256]{1,0:T(8,128)S(1)}, f32[256,256]{0,1:T(8,128)S(1)}, s32[]{:T(128)}, s32[]{:T(128)}) while((s32[]{:T(128)}, f32[256,256]{1,0:T(8,128)S(1)}, f32[256,256]{0,1:T(8,128)S(1)}, s32[]{:T(128)}, s32[]{:T(128)}) %tuple.192), condition=%wide.region_4.5_spmd.clone.clone, body=%wide.region_1.0_spmd.clone.clone.sunk | while | flops 789249 | bytes 277617 | solution.py:30
  976.7 0.9 copy.18
  977.6 390.6 %while.50 = (s32[]{:T(128)}, f32[64,256]{0,1:T(8,128)S(1)}, f32[64,256]{0,1:T(8,128)S(1)}, f32[256,256]{1,0:T(8,128)S(1)}, s32[]{:T(128)}, /*index=5*/s32[]{:T(128)}) while((s32[]{:T(128)}, f32[64,256]{0,1:T(8,128)S(1)}, f32[64,256]{0,1:T(8,128)S(1)}, f32[256,256]{1,0:T(8,128)S(1)}, s32[]{:T(128)}, /*index=5*/s32[]{:T(128)}) %tuple.195), condition=%wide.region_17.18_spmd.clone, body=%wide.region_15.17_spmd.clone.sunk | while | flops 197505 | bytes 138069 | solution.py:44
  1368.3 392.1 %while.52 = (s32[]{:T(128)}, f32[64,256]{0,1:T(8,128)S(1)}, f32[64,256]{0,1:T(8,128)S(1)}, f32[256,256]{0,1:T(8,128)S(1)}, s32[]{:T(128)}, /*index=5*/s32[]{:T(128)}, s32[]{:T(128)}, s32[]{:T(128)}) while((s32[]{:T(128)}, f32[64,256]{0,1:T(8,128)S(1)}, f32[64,256]{0,1:T(8,128)S(1)}, f32[256,256]{0,1:T(8,128)S(1)}, ...), condition=%wide.region_20.21_spmd.clone.clone, body=%wide.region_18.20_spmd.clone.clone.sunk | while | flops 198021 | bytes 71835 | solution.py:55
  1379.7 0.8 fusion.87
  1381.2 0.8 fusion.87
  1382.8 0.8 fusion.87
  1384.3 0.8 fusion.87
  1385.8 0.8 fusion.87
  1387.4 0.8 fusion.87
  1388.9 0.8 fusion.87
  1390.4 0.8 fusion.87
  1391.9 0.8 fusion.87
  1393.5 0.8 fusion.87
  1395.0 0.8 fusion.87
  1396.5 0.8 fusion.87
  1408.8 0.8 fusion.87
  1410.3 0.8 fusion.87
  1411.9 0.8 fusion.87
  1413.4 0.8 fusion.87
  1414.9 0.8 fusion.87
  1416.5 0.8 fusion.87
  (3847 shorter events, 1207.6 us)
Async XLA Ops:
  6.5 29.0 %all-gather.2.cloned.1.call-start = ((), (), s32[]{:S(2)}) async-start(), calls=%async_computation.2 | async-start | bytes 1310720 | tf_op jit(solution)/shard_map/all_gather | solution.py:75
  7.3 78.9 %all-reduce.4.cloned.1.call-start = ((), (), s32[]{:S(2)}) async-start(), calls=%async_computation.5 | async-start | bytes 524288 | tf_op jit(solution)/shard_map/psum | solution.py:88
  9.3 169.1 %reduce-scatter.3.cloned.1.call-start = ((), (), s32[]{:S(2)}) async-start(), calls=%async_computation.3 | async-start | bytes 8650752 | tf_op jit(solution)/shard_map/reduce_scatter | solution.py:96
  68.9 11.3 copy-start.1
  80.2 6.0 copy-start
  86.1 890.6 %reduce-scatter.5.cloned.1.call-start = ((), (), s32[]{:S(2)}) async-start(), calls=%async_computation.4 | async-start | bytes 327680 | tf_op jit(solution)/shard_map/reduce_scatter | solution.py:102
Sparse Core Ops, SparseCore 0:
  9.0 26.4 all-gather.1
  37.9 41.0 all-reduce.3
  86.2 92.1 reduce-scatter.2
  180.6 19.6 reduce-scatter.4
where the time goes:
time: 1780 us; the launch traced here: 1770 us
  other arithmetic  543 us (31%)
  matrix products  500 us (28%)
  loops' own time  364 us (20%)
  local copies, waits for them, and re-layouts  231 us (13%)
  waiting for transfers between devices  113 us (6%)
    another operation x1, loops' own time, factorize(): lax.fori_loop(0, order, column_step, jnp.zeros((order, order), jnp.float32))  347 us
    dot_general x256, matrix products, backward_step(): jnp.dot(solved, below, precision=lax.Precision.HIGHEST)  203 us
    dot_general x256, matrix products, forward_step(): jnp.dot(solved, row_now, precision=lax.Precision.HIGHEST)  202 us
    reduce_sum x256, other arithmetic, forward_step(): pivot = jnp.sum(jnp.where(places == index, row_now, 0.0))  170 us
    reduce_sum x256, other arithmetic, backward_step(): pivot = jnp.sum(jnp.where(places == index, column, 0.0))  170 us
    reduce_sum x256, other arithmetic, column_step(): jnp.sum(jnp.where(places == index, target, 0.0))  169 us
    dynamic_update_slice x256, local copies, waits for them, and re-layouts, column_step(): return lax.dynamic_update_slice_in_dim(lower, column[:, None], index, 1)  157 us
    reduce_scatter x1, waiting for transfers between devices, on_device(): lax.psum_scatter(jnp.einsum('un,nqr->qur', selector, partial_rows, precis...  90.4 us
  transfers between devices with their start and end apart: 4, of which 2 were waited for; matrix products, arithmetic and copies ran while one was open for 28% of the time, Pallas kernels for 0%

commit v1 on v0

v1 whole, which is shorter than its diff:
```python
import functools

import jax
import jax.numpy as jnp
from jax import lax
from jax.experimental import pallas as pl
from jax.experimental.pallas import tpu as pltpu
from jax.sharding import PartitionSpec as P

MESH = pl.DeviceIdType.MESH
PANEL = 32
SUB = 16
CHUNK = 64


def split3(x):
    high = x.astype(jnp.bfloat16)
    rest = x - high.astype(jnp.float32)
    mid = rest.astype(jnp.bfloat16)
    low = (rest - mid.astype(jnp.float32)).astype(jnp.bfloat16)
    return high, mid, low


def small_inverse(cols):
    size = len(cols)
    row = lax.broadcasted_iota(jnp.int32, cols[0].shape, 0)
    cols = list(cols)
    for p in range(size):
        here = row == p
        inv = 1.0 / jnp.broadcast_to(cols[p][p : p + 1], cols[p].shape)
        factor = jnp.where(here, inv, -cols[p] * inv)
        for j in range(size):
            if j == p:
                cols[j] = factor
            else:
                pivot_row = jnp.broadcast_to(cols[j][p : p + 1], cols[j].shape)
                cols[j] = jnp.where(here, 0.0, cols[j]) + factor * pivot_row
    return cols


def combine(cols, rows):
    reps = rows.shape[1] // cols[0].shape[1]
    total = None
    for j, col in enumerate(cols):
        wide = jnp.concatenate([col] * reps, axis=1) if reps > 1 else col
        term = wide * jnp.broadcast_to(rows[j : j + 1], rows.shape)
        total = term if total is None else total + term
    return total


def eliminate(a_ref, k):
    n = a_ref.shape[0]
    base = pl.multiple_of(k * PANEL, PANEL)
    rows = a_ref[pl.ds(base, PANEL), :]
    lane = lax.broadcasted_iota(jnp.int32, (PANEL, n), 1)
    sub = lax.broadcasted_iota(jnp.int32, (PANEL, n), 0)
    inside = (lane >= base) & (lane < base + PANEL)
    eye = jnp.where(lane - base == sub, 1.0, 0.0)
    turned = jnp.where(inside, -eye, jnp.where(lane < base, -rows, rows))
    high, mid, low = split3(turned)
    left = jnp.concatenate([high, high, high, mid, mid, low], axis=0)
    rolled = pltpu.roll(rows, (n - base) % n, 1)
    count = PANEL // SUB
    panel = [rows[s * SUB : (s + 1) * SUB] for s in range(count)]
    diag = [rolled[s * SUB : (s + 1) * SUB, :128] for s in range(count)]
    lane_s, sub_s = lane[:SUB], sub[:SUB]
    lane_d = lax.broadcasted_iota(jnp.int32, (SUB, 128), 1)
    sub_d = lax.broadcasted_iota(jnp.int32, (SUB, 128), 0)
    for s in range(count):
        first = s * SUB
        cols = [
            [jnp.broadcast_to(diag[t][:, first + j : first + j + 1], (SUB, 128)) for j in range(SUB)]
            for t in range(count)
        ]
        inverse = small_inverse(cols[s])
        at = lane_s - base - first
        own = (at >= 0) & (at < SUB)
        at_d = lane_d - first
        own_d = (at_d >= 0) & (at_d < SUB)
        last = s + 1 == count
        fresh = combine(inverse, jnp.where(own, jnp.where(at == sub_s, 1.0, 0.0), panel[s]))
        fresh_d = None
        if not last:
            fresh_d = combine(inverse, jnp.where(own_d, jnp.where(at_d == sub_d, 1.0, 0.0), diag[s]))
        for t in range(count):
            if t != s:
                panel[t] = jnp.where(own, 0.0, panel[t]) - combine(cols[t], fresh)
                if not last:
                    diag[t] = jnp.where(own_d, 0.0, diag[t]) - combine(cols[t], fresh_d)
        panel[s] = fresh
        if not last:
            diag[s] = fresh_d
    solved = jnp.concatenate(panel, axis=0)
    high, mid, low = split3(solved)
    right = jnp.concatenate([high, mid, low, high, mid, high], axis=0)
    update = lax.dot_general(left, right, (((0,), (0,)), ((), ())), preferred_element_type=jnp.float32)
    lane_f = lax.broadcasted_iota(jnp.int32, (n, n), 1)
    a_ref[...] = jnp.where((lane_f >= base) & (lane_f < base + PANEL), 0.0, a_ref[...]) - update
    a_ref[pl.ds(base, PANEL), :] = solved


def block_product(block, item_id, word_id, items, words, item_rows):
    side = block.shape[0]
    rank = words.shape[1]
    item_rows[...] = items[pl.ds(item_id * side, side), :].astype(jnp.float32)
    word_rows = words[pl.ds(word_id * side, side), :]

    def step(c, total):
        terms = []
        for j in range(CHUNK):
            row = jnp.broadcast_to(item_rows[pl.ds(c * CHUNK + j, 1), :], (side, rank))
            terms.append(word_rows * row.astype(jnp.bfloat16))
        khatri = jnp.concatenate(terms, axis=0)
        values = block[:, pl.ds(pl.multiple_of(c * CHUNK * side, CHUNK * side), CHUNK * side)]
        return total + jnp.dot(values, khatri, preferred_element_type=jnp.float32)

    return lax.fori_loop(0, side // CHUNK, step, jnp.zeros((side, rank), jnp.float32))


def gram_of(rows):
    return lax.dot_general(rows, rows, (((0,), (0,)), ((), ())), preferred_element_type=jnp.float32)


def kernel(
    groups, owners, local_u,
    user_ids, item_ids, word_ids, blocks_hbm, item_hbm, word_hbm, out_ref,
    blocks, items, words, item_rows, part, gram, send, recv, mine, theirs, ids_send, ids_recv, select,
    block_sem, word_sem, item_sem, gather_send, gather_recv, pass_send, pass_recv,
    ids_ssem, ids_rsem, rows_ssem, rows_rsem, z_send, z_recv,
):
    nblocks, side = blocks.shape[0], blocks.shape[1]
    rank = words.shape[1]
    share = side // owners
    message = nblocks * share
    halves = rank // 128
    held = item_hbm.shape[0]
    half = held // 2
    group = lax.axis_index("blk")
    owner = lax.axis_index("own")
    core = owner % 2
    sibling = owner + 1 - 2 * core

    word_copy = pltpu.make_async_copy(word_hbm, words, word_sem)
    word_copy.start()
    mine_at = pl.multiple_of(group * held, held)
    item_copy = pltpu.make_async_copy(item_hbm, items.at[pl.ds(mine_at, held)], item_sem)
    item_copy.start()

    barrier = pltpu.get_barrier_semaphore()
    for d in range(1, groups):
        pl.semaphore_signal(barrier, inc=1, device_id=((group + d) % groups, owner), device_id_type=MESH)

    def greet(d, carry):
        pl.semaphore_signal(barrier, inc=1, device_id=(group, (owner + d) % owners), device_id_type=MESH)
        return carry

    lax.fori_loop(1, owners, greet, 0)
    pl.semaphore_wait(barrier, groups - 1 + owners - 1)

    def gather_copy(d, source_group):
        start = pl.multiple_of(source_group * held + core * half, half)
        return pltpu.make_async_remote_copy(
            src_ref=item_hbm.at[pl.ds(pl.multiple_of(core * half, half), half)],
            dst_ref=items.at[pl.ds(start, half)],
            send_sem=gather_send.at[d - 1],
            recv_sem=gather_recv.at[d - 1],
            device_id=((group + d) % groups, owner),
            device_id_type=MESH,
        )

    gathers = {d: gather_copy(d, group) for d in range(1, groups)}
    for d in (2, 1, 3):
        gathers[d].start()
    for n in range(nblocks):
        pltpu.make_async_copy(blocks_hbm.at[n], blocks.at[n], block_sem.at[n]).start()

    for n in range(nblocks):
        ids_send[n * share : (n + 1) * share, :] = jnp.full((share, ids_send.shape[1]), user_ids[n], jnp.int32)
    own_ids = pltpu.make_async_copy(ids_send, ids_recv.at[owner], ids_rsem)
    own_ids.start()

    def send_ids(d, carry):
        pltpu.make_async_remote_copy(
            src_ref=ids_send, dst_ref=ids_recv.at[owner], send_sem=ids_ssem, recv_sem=ids_rsem,
            device_id=(group, (owner + d) % owners), device_id_type=MESH,
        ).start()
        return carry

    lax.fori_loop(1, owners, send_ids, 0)

    word_copy.wait()
    gram_words = gram_of(words[...])

    def pass_copy(d):
        start = pl.multiple_of((group + groups - d) % groups * held + core * half, half)
        return pltpu.make_async_remote_copy(
            src_ref=items.at[pl.ds(start, half)],
            dst_ref=items.at[pl.ds(start, half)],
            send_sem=pass_send.at[d - 1],
            recv_sem=pass_recv.at[d - 1],
            device_id=(group, sibling),
            device_id_type=MESH,
        )

    passes = {}
    for d in (1, 3, 2):
        gathers[d].wait_recv()
        passes[d] = pass_copy(d)
        passes[d].start()

    pltpu.make_async_copy(ids_recv, ids_recv, ids_rsem).wait()
    rows_in = owners * message
    rows_out = groups * share * local_u
    ids = ids_recv[...].reshape(rows_in, ids_recv.shape[2])
    parts = []
    for h in range(rows_out // 128):
        to = lax.broadcasted_iota(jnp.int32, (rows_in, 128), 1) + h * 128
        source = lax.broadcasted_iota(jnp.int32, (rows_in, 128), 0)
        to_user = to // (share * local_u) * local_u + to % local_u
        hit = (ids == to_user) & (source % share == to // local_u % share)
        parts.append(jnp.where(hit, 1.0, 0.0).astype(jnp.bfloat16))
    select[...] = jnp.concatenate(parts, axis=1).T

    item_copy.wait()
    for d in (1, 3, 2):
        passes[d].wait_recv()

    pair = 2 * share

    def row_copy(t, to):
        return pltpu.make_async_remote_copy(
            src_ref=send.at[:, pl.ds(pl.multiple_of(to * message + t * pair, pair), pair)],
            dst_ref=recv.at[:, pl.ds(pl.multiple_of(owner * message + t * pair, pair), pair)],
            send_sem=rows_ssem, recv_sem=rows_rsem,
            device_id=(group, to), device_id_type=MESH,
        )

    def product_step(n, carry):
        pltpu.make_async_copy(blocks_hbm.at[n], blocks.at[n], block_sem.at[n]).wait()
        product = block_product(blocks.at[n], item_ids[n], word_ids[n], items, words, item_rows)
        for h in range(halves):
            part[h] = product[:, h * 128 : (h + 1) * 128]
            for row in range(share):
                to_rows = pl.ds(n * share + row, owners, stride=message)
                send[h, to_rows, :] = part[h, pl.ds(row, owners, stride=share), :]

        @pl.when(n % 2 == 1)
        def _():
            def send_rows(d, inner):
                row_copy(n // 2, (owner + d) % owners).start()
                return inner

            lax.fori_loop(1, owners, send_rows, 0)

        return carry

    lax.fori_loop(0, nblocks, product_step, 0)
    mine_rows = pl.ds(pl.multiple_of(owner * message, message), message)
    pltpu.make_async_copy(send.at[:, mine_rows], recv.at[:, mine_rows], rows_rsem).start()

    gram[...] = gram_of(items[...]) * gram_words
    steps = rank // PANEL

    def eliminate_step(k, carry):
        eliminate(gram, k)
        return carry

    lax.fori_loop(0, steps // 2, eliminate_step, 0)

    pltpu.make_async_copy(recv, recv, rows_rsem).wait()
    high, mid, low = split3(jnp.concatenate([recv[h] for h in range(halves)], axis=1))
    chosen = select[...]
    total = jnp.dot(chosen, high, preferred_element_type=jnp.float32)
    total += jnp.dot(chosen, mid, preferred_element_type=jnp.float32)
    total += jnp.dot(chosen, low, preferred_element_type=jnp.float32)
    mine[...] = total
    count = share * local_u

    def z_copy(d):
        to = (group + d) % groups
        return pltpu.make_async_remote_copy(
            src_ref=mine.at[pl.ds(pl.multiple_of(to * count, count), count)],
            dst_ref=theirs.at[d - 1],
            send_sem=z_send.at[d - 1], recv_sem=z_recv.at[d - 1],
            device_id=(to, owner), device_id_type=MESH,
        )

    zs = [z_copy(d) for d in range(1, groups)]
    for z in zs:
        z.start()

    lax.fori_loop(steps // 2, steps, eliminate_step, 0)

    rows = mine[pl.ds(pl.multiple_of(group * count, count), count), :]
    for d in range(1, groups):
        zs[d - 1].wait_recv()
        rows = rows + theirs[d - 1]
    solved = jnp.dot(rows, gram[...], preferred_element_type=jnp.float32, precision=lax.Precision.HIGHEST)
    out_ref[...] = solved.reshape(out_ref.shape)

    for d in range(1, groups):
        gathers[d].wait_send()
        passes[d].wait_send()
        zs[d - 1].wait_send()
    other_ids = ids_recv.at[pl.ds(0, owners - 1)]
    pltpu.make_async_copy(other_ids, other_ids, ids_ssem).wait()
    other_rows = send.at[:, pl.ds(0, (owners - 1) * message)]
    pltpu.make_async_copy(other_rows, other_rows, rows_ssem).wait()


def solution(mesh):
    groups, owners = mesh.shape["blk"], mesh.shape["own"]

    def on_device(blocks, user_block, item_block, word_block, item_factor, word_factor):
        nblocks, side, _ = blocks.shape
        rank = item_factor.shape[1]
        share = side // owners
        message = nblocks * share
        local_u = nblocks * owners // 8
        count = share * local_u
        dma = pltpu.SemaphoreType.DMA
        smem = pl.BlockSpec(memory_space=pltpu.SMEM)
        hbm = pl.BlockSpec(memory_space=pl.ANY)
        return pl.pallas_call(
            functools.partial(kernel, groups, owners, local_u),
            out_shape=jax.ShapeDtypeStruct((share, local_u, rank), jnp.float32),
            in_specs=[smem, smem, smem, hbm, hbm, hbm],
            out_specs=pl.BlockSpec(memory_space=pltpu.VMEM),
            scratch_shapes=[
                pltpu.VMEM(blocks.shape, jnp.bfloat16),
                pltpu.VMEM((groups * item_factor.shape[0], rank), jnp.bfloat16),
                pltpu.VMEM(word_factor.shape, jnp.bfloat16),
                pltpu.VMEM((side, rank), jnp.float32),
                pltpu.VMEM((rank // 128, side, 128), jnp.float32),
                pltpu.VMEM((rank, rank), jnp.float32),
                pltpu.VMEM((rank // 128, owners * message, 128), jnp.float32),
                pltpu.VMEM((rank // 128, owners * message, 128), jnp.float32),
                pltpu.VMEM((groups * count, rank), jnp.float32),
                pltpu.VMEM((groups - 1, count, rank), jnp.float32),
                pltpu.VMEM((message, 128), jnp.int32),
                pltpu.VMEM((owners, message, 128), jnp.int32),
                pltpu.VMEM((groups * count, owners * message), jnp.bfloat16),
                dma((nblocks,)), dma, dma,
                dma((groups - 1,)), dma((groups - 1,)), dma((groups - 1,)), dma((groups - 1,)),
                dma, dma, dma, dma,
                dma((groups - 1,)), dma((groups - 1,)),
            ],
            compiler_params=pltpu.CompilerParams(
                collective_id=0, has_side_effects=True, vmem_limit_bytes=56 * 2**20
            ),
            name="als_user_update",
        )(user_block, item_block, word_block, blocks, item_factor, word_factor)

    return jax.shard_map(
        on_device,
        mesh=mesh,
        in_specs=(
            P(("blk", "own"), None, None),
            P(("blk", "own")),
            P(("blk", "own")),
            P(("blk", "own")),
            P("blk", None),
            P(),
        ),
        out_specs=P("own", "blk", None),
        check_vma=False,
    )
```

time: 1780 us -> 40.6 us (0.02)
  other arithmetic: 543 us -> 0 us
  matrix products: 500 us -> 0 us
  loops' own time: 364 us -> 0 us
  local copies, waits for them, and re-layouts: 231 us -> 1.47 us
  waiting for transfers between devices: 113 us -> 0 us
  Pallas kernels: 0 us -> 38.9 us
    reduce_sum x768 -> x0, other arithmetic: 510 us -> none  [the longest x256 170 us: forward_step(): pivot = jnp.sum(jnp.where(places == index, row_now, 0.0))]
    dot_general x775 -> x0, matrix products: 500 us -> none  [the longest x256 203 us: backward_step(): jnp.dot(solved, below, precision=lax.Precision.HIGHEST)]
    another operation x7 -> x0, loops' own time: 364 us -> none  [the longest x1 347 us: factorize(): lax.fori_loop(0, order, column_step, jnp.zeros((order, order), jnp.float32))]
    dynamic_update_slice x768 -> x0, local copies, waits for them, and re-layouts: 176 us -> none  [the longest x256 157 us: column_step(): return lax.dynamic_update_slice_in_dim(lower, column[:, None], index, 1)]
    reduce_scatter x2 -> x0, waiting for transfers between devices: 90.4 us -> none  [the longest x1 90.4 us: on_device(): lax.psum_scatter(jnp.einsum('un,nqr->qur', selector, partial_rows, precis...]
    pallas_call x0 -> x1, Pallas kernels: none -> 38.9 us  [on_device(): pl.pallas_call(functools.partial(kernel, groups, owners, local_u), out_sh...]
    broadcast_in_dim x257 -> x0, local copies, waits for them, and re-layouts: 36 us -> none  [the longest x256 36 us: column_step(): return lax.dynamic_update_slice_in_dim(lower, column[:, None], index, 1)]
    all_gather x1 -> x0, waiting for transfers between devices: 22.2 us -> none  [on_device(): piece = lax.all_gather(item_factor, 'blk', axis=0, tiled=True)]
  transfers between devices with their start and end apart: 4 -> 0, of which waited for: 2 -> 0; matrix products, arithmetic and copies ran while one was open for 28% -> 0% of each run, Pallas kernels for 0% -> 0%
where the time goes in v1:
time: 40.6 us; the launch traced here: 40.4 us
  Pallas kernels  38.9 us (96%)
  local copies, waits for them, and re-layouts  1.47 us (4%)
    pallas_call x1, Pallas kernels, on_device(): pl.pallas_call(functools.partial(kernel, groups, owners, local_u), out_sh...  38.9 us
    unnamed x1, local copies, waits for them, and re-layouts  1.47 us

profile of v1, /device:TPU:1, one launch (start us, length us, event | category | flops | bytes accessed | tf_op | source)
XLA Modules:
  0.0 40.4 jit_solution(9680350401130400906)
XLA Ops:
  0.0 38.9 %als_user_update.1 = f32[4,16,256]{2,1,0:T(8,128)} custom-call(s32[4]{0:T(128)} %user_ids.1, s32[4]{0:T(128)} %item_ids.1, s32[4]{0:T(128)} %word_ids.1, bf16[4,128,16384]{2,1,0:T(8,128)(2,1)} %blocks_hbm.1, bf16[512,256]{1,0:T(8,128)(2,1)} %item_hbm.1, bf16[4096,256]{1,0:T(8,128)(2,1)} %word_hbm.1), custom_call_target="tpu_custom_call" | custom-call | tf_op jit(solution)/shard_map/als_user_update/pallas_call | solution.py:324
  38.9 1.5 %copy.8 = f32[4,16,256]{2,1,0:T(8,128)} copy(f32[4,16,256]{2,1,0:T(8,128)} %als_user_update.1) | data formatting | bytes 131072

commit v2 on v1

--- a/solution.py
+++ b/solution.py
@@ -10,7 +10,7 @@
 MESH = pl.DeviceIdType.MESH
 PANEL = 32
 SUB = 16
-CHUNK = 64
+CHUNK = 128
 
 
 def split3(x):
@@ -155,6 +155,8 @@
         return carry
 
     lax.fori_loop(1, owners, greet, 0)
+    for n in range(nblocks):
+        pltpu.make_async_copy(blocks_hbm.at[n], blocks.at[n], block_sem.at[n]).start()
     pl.semaphore_wait(barrier, groups - 1 + owners - 1)
 
     def gather_copy(d, source_group):
@@ -171,8 +173,6 @@
     gathers = {d: gather_copy(d, group) for d in range(1, groups)}
     for d in (2, 1, 3):
         gathers[d].start()
-    for n in range(nblocks):
-        pltpu.make_async_copy(blocks_hbm.at[n], blocks.at[n], block_sem.at[n]).start()
 
     for n in range(nblocks):
         ids_send[n * share : (n + 1) * share, :] = jnp.full((share, ids_send.shape[1]), user_ids[n], jnp.int32)
@@ -207,6 +207,43 @@
         gathers[d].wait_recv()
         passes[d] = pass_copy(d)
         passes[d].start()
+
+    item_copy.wait()
+    for d in (1, 3, 2):
+        passes[d].wait_recv()
+
+    pair = 2 * share
+
+    def row_copy(t, to):
+        return pltpu.make_async_remote_copy(
+            src_ref=send.at[:, pl.ds(pl.multiple_of(to * message + t * pair, pair), pair)],
+            dst_ref=recv.at[:, pl.ds(pl.multiple_of(owner * message + t * pair, pair), pair)],
+            send_sem=rows_ssem, recv_sem=rows_rsem,
+            device_id=(group, to), device_id_type=MESH,
+        )
+
+    def product_step(n, carry):
+        pltpu.make_async_copy(blocks_hbm.at[n], blocks.at[n], block_sem.at[n]).wait()
+        product = block_product(blocks.at[n], item_ids[n], word_ids[n], items, words, item_rows)
+        for h in range(halves):
+            part[h] = product[:, h * 128 : (h + 1) * 128]
+            for row in range(share):
+                to_rows = pl.ds(n * share + row, owners, stride=message)
+                send[h, to_rows, :] = part[h, pl.ds(row, owners, stride=share), :]
+
+        @pl.when(n % 2 == 1)
+        def _():
+            def send_rows(d, inner):
+                row_copy(n // 2, (owner + d) % owners).start()
+                return inner
+
+            lax.fori_loop(1, owners, send_rows, 0)
+
+        return carry
+
+    lax.fori_loop(0, nblocks, product_step, 0)
+    mine_rows = pl.ds(pl.multiple_of(owner * message, message), message)
+    pltpu.make_async_copy(send.at[:, mine_rows], recv.at[:, mine_rows], rows_rsem).start()
 
     pltpu.make_async_copy(ids_recv, ids_recv, ids_rsem).wait()
     rows_in = owners * message
@@ -220,43 +257,6 @@
         hit = (ids == to_user) & (source % share == to // local_u % share)
         parts.append(jnp.where(hit, 1.0, 0.0).astype(jnp.bfloat16))
     select[...] = jnp.concatenate(parts, axis=1).T
-
-    item_copy.wait()
-    for d in (1, 3, 2):
-        passes[d].wait_recv()
-
-    pair = 2 * share
-
-    def row_copy(t, to):
-        return pltpu.make_async_remote_copy(
-            src_ref=send.at[:, pl.ds(pl.multiple_of(to * message + t * pair, pair), pair)],
-            dst_ref=recv.at[:, pl.ds(pl.multiple_of(owner * message + t * pair, pair), pair)],
-            send_sem=rows_ssem, recv_sem=rows_rsem,
-            device_id=(group, to), device_id_type=MESH,
-        )
-
-    def product_step(n, carry):
-        pltpu.make_async_copy(blocks_hbm.at[n], blocks.at[n], block_sem.at[n]).wait()
-        product = block_product(blocks.at[n], item_ids[n], word_ids[n], items, words, item_rows)
-        for h in range(halves):
-            part[h] = product[:, h * 128 : (h + 1) * 128]
-            for row in range(share):
-                to_rows = pl.ds(n * share + row, owners, stride=message)
-                send[h, to_rows, :] = part[h, pl.ds(row, owners, stride=share), :]
-
-        @pl.when(n % 2 == 1)
-        def _():
-            def send_rows(d, inner):
-                row_copy(n // 2, (owner + d) % owners).start()
-                return inner
-
-            lax.fori_loop(1, owners, send_rows, 0)
-
-        return carry
-
-    lax.fori_loop(0, nblocks, product_step, 0)
-    mine_rows = pl.ds(pl.multiple_of(owner * message, message), message)
-    pltpu.make_async_copy(send.at[:, mine_rows], recv.at[:, mine_rows], rows_rsem).start()
 
     gram[...] = gram_of(items[...]) * gram_words
     steps = rank // PANEL

time: 40.6 us -> 39.6 us (0.975)
  Pallas kernels: 38.9 us -> 38 us
    pallas_call x1, Pallas kernels: 38.9 us -> 38 us  [on_device(): pl.pallas_call(functools.partial(kernel, groups, owners, local_u), out_sh...]
where the time goes in v2:
time: 39.6 us; the launch traced here: 39.5 us
  Pallas kernels  38 us (96%)
  local copies, waits for them, and re-layouts  1.47 us (4%)
    pallas_call x1, Pallas kernels, on_device(): pl.pallas_call(functools.partial(kernel, groups, owners, local_u), out_sh...  38 us
    unnamed x1, local copies, waits for them, and re-layouts  1.47 us

profile of v2, /device:TPU:1, one launch (start us, length us, event | category | flops | bytes accessed | tf_op | source)
XLA Modules:
  0.0 39.5 jit_solution(4958177953479038926)
XLA Ops:
  0.0 38.0 %als_user_update.1 = f32[4,16,256]{2,1,0:T(8,128)} custom-call(s32[4]{0:T(128)} %user_ids.1, s32[4]{0:T(128)} %item_ids.1, s32[4]{0:T(128)} %word_ids.1, bf16[4,128,16384]{2,1,0:T(8,128)(2,1)} %blocks_hbm.1, bf16[512,256]{1,0:T(8,128)(2,1)} %item_hbm.1, bf16[4096,256]{1,0:T(8,128)(2,1)} %word_hbm.1), custom_call_target="tpu_custom_call" | custom-call | tf_op jit(solution)/shard_map/als_user_update/pallas_call | solution.py:324
  38.0 1.5 %copy.8 = f32[4,16,256]{2,1,0:T(8,128)} copy(f32[4,16,256]{2,1,0:T(8,128)} %als_user_update.1) | data formatting | bytes 131072

commit v3 on v2

--- a/solution.py
+++ b/solution.py
@@ -159,20 +159,24 @@
         pltpu.make_async_copy(blocks_hbm.at[n], blocks.at[n], block_sem.at[n]).start()
     pl.semaphore_wait(barrier, groups - 1 + owners - 1)
 
-    def gather_copy(d, source_group):
-        start = pl.multiple_of(source_group * held + core * half, half)
+    quarter = half // 2
+    pieces = ((1, 0, half), (3, 0, half), (2, 0, quarter), (2, quarter, quarter))
+
+    def gather_copy(i):
+        d, first, length = pieces[i]
+        start = pl.multiple_of(group * held + core * half + first, quarter)
         return pltpu.make_async_remote_copy(
-            src_ref=item_hbm.at[pl.ds(pl.multiple_of(core * half, half), half)],
-            dst_ref=items.at[pl.ds(start, half)],
-            send_sem=gather_send.at[d - 1],
-            recv_sem=gather_recv.at[d - 1],
+            src_ref=item_hbm.at[pl.ds(pl.multiple_of(core * half + first, quarter), length)],
+            dst_ref=items.at[pl.ds(start, length)],
+            send_sem=gather_send.at[i],
+            recv_sem=gather_recv.at[i],
             device_id=((group + d) % groups, owner),
             device_id_type=MESH,
         )
 
-    gathers = {d: gather_copy(d, group) for d in range(1, groups)}
-    for d in (2, 1, 3):
-        gathers[d].start()
+    gathers = [gather_copy(i) for i in range(len(pieces))]
+    for i in (2, 0, 1, 3):
+        gathers[i].start()
 
     for n in range(nblocks):
         ids_send[n * share : (n + 1) * share, :] = jnp.full((share, ids_send.shape[1]), user_ids[n], jnp.int32)
@@ -191,26 +195,26 @@
     word_copy.wait()
     gram_words = gram_of(words[...])
 
-    def pass_copy(d):
-        start = pl.multiple_of((group + groups - d) % groups * held + core * half, half)
+    def pass_copy(i):
+        d, first, length = pieces[i]
+        start = pl.multiple_of((group + groups - d) % groups * held + core * half + first, quarter)
         return pltpu.make_async_remote_copy(
-            src_ref=items.at[pl.ds(start, half)],
-            dst_ref=items.at[pl.ds(start, half)],
-            send_sem=pass_send.at[d - 1],
-            recv_sem=pass_recv.at[d - 1],
+            src_ref=items.at[pl.ds(start, length)],
+            dst_ref=items.at[pl.ds(start, length)],
+            send_sem=pass_send.at[i],
+            recv_sem=pass_recv.at[i],
             device_id=(group, sibling),
             device_id_type=MESH,
         )
 
-    passes = {}
-    for d in (1, 3, 2):
-        gathers[d].wait_recv()
-        passes[d] = pass_copy(d)
-        passes[d].start()
+    passes = [pass_copy(i) for i in range(len(pieces))]
+    for gather, shared in zip(gathers, passes):
+        gather.wait_recv()
+        shared.start()
 
     item_copy.wait()
-    for d in (1, 3, 2):
-        passes[d].wait_recv()
+    for shared in passes:
+        shared.wait_recv()
 
     pair = 2 * share
 
@@ -298,10 +302,8 @@
     solved = jnp.dot(rows, gram[...], preferred_element_type=jnp.float32, precision=lax.Precision.HIGHEST)
     out_ref[...] = solved.reshape(out_ref.shape)
 
-    for d in range(1, groups):
-        gathers[d].wait_send()
-        passes[d].wait_send()
-        zs[d - 1].wait_send()
+    for sent in gathers + passes + zs:
+        sent.wait_send()
     other_ids = ids_recv.at[pl.ds(0, owners - 1)]
     pltpu.make_async_copy(other_ids, other_ids, ids_ssem).wait()
     other_rows = send.at[:, pl.ds(0, (owners - 1) * message)]
@@ -341,7 +343,7 @@
                 pltpu.VMEM((owners, message, 128), jnp.int32),
                 pltpu.VMEM((groups * count, owners * message), jnp.bfloat16),
                 dma((nblocks,)), dma, dma,
-                dma((groups - 1,)), dma((groups - 1,)), dma((groups - 1,)), dma((groups - 1,)),
+                dma((4,)), dma((4,)), dma((4,)), dma((4,)),
                 dma, dma, dma, dma,
                 dma((groups - 1,)), dma((groups - 1,)),
             ],

time: 39.6 us -> 39.2 us (0.990)
  Pallas kernels: 38 us -> 37.5 us
    pallas_call x1, Pallas kernels: 38 us -> 37.5 us  [on_device(): pl.pallas_call(functools.partial(kernel, groups, owners, local_u), out_sh...]
where the time goes in v3:
time: 39.2 us; the launch traced here: 39 us
  Pallas kernels  37.5 us (96%)
  local copies, waits for them, and re-layouts  1.47 us (4%)
    pallas_call x1, Pallas kernels, on_device(): pl.pallas_call(functools.partial(kernel, groups, owners, local_u), out_sh...  37.5 us
    unnamed x1, local copies, waits for them, and re-layouts  1.47 us

profile of v3, /device:TPU:1, one launch (start us, length us, event | category | flops | bytes accessed | tf_op | source)
XLA Modules:
  0.0 39.0 jit_solution(2638870750171561039)
XLA Ops:
  0.0 37.5 %als_user_update.1 = f32[4,16,256]{2,1,0:T(8,128)} custom-call(s32[4]{0:T(128)} %user_ids.1, s32[4]{0:T(128)} %item_ids.1, s32[4]{0:T(128)} %word_ids.1, bf16[4,128,16384]{2,1,0:T(8,128)(2,1)} %blocks_hbm.1, bf16[512,256]{1,0:T(8,128)(2,1)} %item_hbm.1, bf16[4096,256]{1,0:T(8,128)(2,1)} %word_hbm.1), custom_call_target="tpu_custom_call" | custom-call | tf_op jit(solution)/shard_map/als_user_update/pallas_call | solution.py:326
  37.6 1.5 %copy.8 = f32[4,16,256]{2,1,0:T(8,128)} copy(f32[4,16,256]{2,1,0:T(8,128)} %als_user_update.1) | data formatting | bytes 131072

commit v4 on v3

--- a/solution.py
+++ b/solution.py
@@ -178,20 +178,6 @@
     for i in (2, 0, 1, 3):
         gathers[i].start()
 
-    for n in range(nblocks):
-        ids_send[n * share : (n + 1) * share, :] = jnp.full((share, ids_send.shape[1]), user_ids[n], jnp.int32)
-    own_ids = pltpu.make_async_copy(ids_send, ids_recv.at[owner], ids_rsem)
-    own_ids.start()
-
-    def send_ids(d, carry):
-        pltpu.make_async_remote_copy(
-            src_ref=ids_send, dst_ref=ids_recv.at[owner], send_sem=ids_ssem, recv_sem=ids_rsem,
-            device_id=(group, (owner + d) % owners), device_id_type=MESH,
-        ).start()
-        return carry
-
-    lax.fori_loop(1, owners, send_ids, 0)
-
     word_copy.wait()
     gram_words = gram_of(words[...])
 
@@ -211,6 +197,20 @@
     for gather, shared in zip(gathers, passes):
         gather.wait_recv()
         shared.start()
+
+    for n in range(nblocks):
+        ids_send[n * share : (n + 1) * share, :] = jnp.full((share, ids_send.shape[1]), user_ids[n], jnp.int32)
+    own_ids = pltpu.make_async_copy(ids_send, ids_recv.at[owner], ids_rsem)
+    own_ids.start()
+
+    def send_ids(d, carry):
+        pltpu.make_async_remote_copy(
+            src_ref=ids_send, dst_ref=ids_recv.at[owner], send_sem=ids_ssem, recv_sem=ids_rsem,
+            device_id=(group, (owner + d) % owners), device_id_type=MESH,
+        ).start()
+        return carry
+
+    lax.fori_loop(1, owners, send_ids, 0)
 
     item_copy.wait()
     for shared in passes:

time: 39.2 us -> 39.2 us (level)
  no operation moved by 1% of the time
where the time goes in v4:
time: 39.2 us; the launch traced here: 39.1 us
  Pallas kernels  37.6 us (96%)
  local copies, waits for them, and re-layouts  1.47 us (4%)
    pallas_call x1, Pallas kernels, on_device(): pl.pallas_call(functools.partial(kernel, groups, owners, local_u), out_sh...  37.6 us
    unnamed x1, local copies, waits for them, and re-layouts  1.47 us

profile of v4, /device:TPU:1, one launch (start us, length us, event | category | flops | bytes accessed | tf_op | source)
XLA Modules:
  0.0 39.1 jit_solution(3811803836910774882)
XLA Ops:
  0.0 37.6 %als_user_update.1 = f32[4,16,256]{2,1,0:T(8,128)} custom-call(s32[4]{0:T(128)} %user_ids.1, s32[4]{0:T(128)} %item_ids.1, s32[4]{0:T(128)} %word_ids.1, bf16[4,128,16384]{2,1,0:T(8,128)(2,1)} %blocks_hbm.1, bf16[512,256]{1,0:T(8,128)(2,1)} %item_hbm.1, bf16[4096,256]{1,0:T(8,128)(2,1)} %word_hbm.1), custom_call_target="tpu_custom_call" | custom-call | tf_op jit(solution)/shard_map/als_user_update/pallas_call | solution.py:326
  37.6 1.5 %copy.8 = f32[4,16,256]{2,1,0:T(8,128)} copy(f32[4,16,256]{2,1,0:T(8,128)} %als_user_update.1) | data formatting | bytes 131072
